TPU v7x, 32 devices: a whole 2x2x4 slice. The times are simulated.
32 devices in a mesh: rep: 16 (over z, y, core), shard: 2 (over x).
Axes of the slice: x: 2, y: 2, z: 4, core: 2. Of those that a mesh axis runs over, the one named last changes fastest.
Arguments:
- tokens: bfloat16 [32768, 768], P(('rep', 'shard')), may hold values from -6 to 6
- image_ids: int32 [32, 1024], P(('rep', 'shard')), may hold values from 0 to 7, never falling along the last dimension, each value on 1 to 256 neighbouring positions
- ln1_gain: bfloat16 [768], P('shard'), may hold values from 0.5 to 1.5
- ln1_bias: bfloat16 [768], P('shard'), may hold values from -3 to 3
- w_query: bfloat16 [768, 768], P('shard'), may hold values from -0.21875 to 0.21875
- w_key: bfloat16 [768, 768], P('shard'), may hold values from -0.21875 to 0.21875
- w_value: bfloat16 [768, 768], P('shard'), may hold values from -0.21875 to 0.21875
- b_value: bfloat16 [768], P('shard'), may hold values from -3 to 3
- q_gain: bfloat16 [768], P('shard'), may hold values from 0.796875 to 1.59375
- k_gain: bfloat16 [768], P('shard'), may hold values from 0.796875 to 1.59375
- w_out: bfloat16 [768, 768], P('shard'), may hold values from -0.875 to 0.875
- b_out: bfloat16 [768], P('shard'), may hold values from -3 to 3
- ln2_gain: bfloat16 [768], P('shard'), may hold values from 0.5 to 1.5
- ln2_bias: bfloat16 [768], P('shard'), may hold values from -3 to 3
- w_up: bfloat16 [768, 3072], P('shard'), may hold values from -0.21875 to 0.21875
- b_up: bfloat16 [3072], P('shard'), may hold values from -3 to 3
- w_down: bfloat16 [3072, 768], P('shard'), may hold values from -0.15625 to 0.15625
- b_down: bfloat16 [768], P('shard'), may hold values from -3 to 3
- cotangent: bfloat16 [32768, 768], P(('rep', 'shard')), may hold values from -6 to 6
Outputs:
- outputs: bfloat16 [32768, 768], P(('rep', 'shard'))
- d_tokens: bfloat16 [32768, 768], P(('rep', 'shard'))
- g_ln1_gain: float32 [768], P('shard')
- g_ln1_bias: float32 [768], P('shard')
- g_w_query: float32 [768, 768], P('shard')
- g_w_key: float32 [768, 768], P('shard')
- g_w_value: float32 [768, 768], P('shard')
- g_b_value: float32 [768], P('shard')
- g_q_gain: float32 [768], P('shard')
- g_k_gain: float32 [768], P('shard')
- g_w_out: float32 [768, 768], P('shard')
- g_b_out: float32 [768], P('shard')
- g_ln2_gain: float32 [768], P('shard')
- g_ln2_bias: float32 [768], P('shard')
- g_w_up: float32 [768, 3072], P('shard')
- g_b_up: float32 [3072], P('shard')
- g_w_down: float32 [3072, 768], P('shard')
- g_b_down: float32 [768], P('shard')
Inputs may be any that keep to these rules, and one draw needn't show every extreme that they name: `image_ids`: each row is one packed sequence: ids never fall along the row, each image has 1 to 256 tokens, one exactly 256, and a row holds 8 images.
All inputs are finite; a program needn't handle non-finite values.
Results may differ from a plain program's by a relative error of at most 0.012.
Values may be sent and summed in bfloat16 or wider, within the bound.
A program may use at most 192 MiB of HBM per device.

v0:
```python
from functools import partial
import math

import jax
import jax.numpy as jnp
from jax import lax
from jax.sharding import PartitionSpec as P

D = 768
HEADS = 12


EPS = 1e-06


def norm_rows(value, gain, bias):
    centre = value - jnp.mean(value, -1, keepdims=True)
    spread = jnp.mean(centre * centre, -1, keepdims=True)
    return centre * lax.rsqrt(spread + EPS) * gain + bias


def norm_heads(value, gain):
    rows = value.shape[0]
    split = value.reshape(rows, HEADS, D // HEADS)
    centre = split - jnp.mean(split, -1, keepdims=True)
    spread = jnp.mean(centre * centre, -1, keepdims=True)
    return (centre * lax.rsqrt(spread + EPS)).reshape(rows, D) * gain


def product(left, right):
    return jnp.dot(left, right, preferred_element_type=jnp.float32)


def contract_rows(left, right):
    return lax.dot_general(
        left, right, (((0,), (0,)), ((), ())), preferred_element_type=jnp.float32
    )


def contract_cols(left, right):
    return lax.dot_general(
        left, right, (((1,), (1,)), ((), ())), preferred_element_type=jnp.float32
    )


def split_heads(value):
    return value.reshape(value.shape[0], HEADS, D // HEADS).transpose(1, 0, 2)


def merge_heads(value):
    return value.transpose(1, 0, 2).reshape(value.shape[1], D)


def head_forward(query, key, values, allowed):
    scale = 1.0 / math.sqrt(D // HEADS)
    scores = jnp.where(allowed, contract_cols(query, key) * scale, -1e30)
    peak = jnp.max(scores, -1, keepdims=True)
    expo = jnp.exp(scores - peak)
    total = jnp.sum(expo, -1, keepdims=True)
    probs = (expo / total).astype(jnp.bfloat16)
    context = product(probs, values).astype(jnp.bfloat16)
    return (context, (peak + jnp.log(total))[:, 0])


def head_backward(query, key, values, d_context, logsum, allowed):
    scale = 1.0 / math.sqrt(D // HEADS)
    scores = jnp.where(allowed, contract_cols(query, key) * scale, -1e30)
    probs = jnp.exp(scores - logsum[:, None])
    d_values = contract_rows(probs.astype(jnp.bfloat16), d_context)
    d_probs = contract_cols(d_context, values)
    d_scores = (probs * (d_probs - jnp.sum(probs * d_probs, -1, keepdims=True))).astype(
        jnp.bfloat16
    )
    d_query = product(d_scores, key) * scale
    d_key = contract_rows(d_scores, query) * scale
    return (d_query, d_key, d_values)


def on_device(
    tokens,
    image_ids,
    ln1_gain,
    ln1_bias,
    w_query,
    w_key,
    w_value,
    b_value,
    q_gain,
    k_gain,
    w_out,
    b_out,
    ln2_gain,
    ln2_bias,
    w_up,
    b_up,
    w_down,
    b_down,
    cotangent,
):
    full = (
        lax.all_gather(ln1_gain, "shard", axis=0, tiled=True),
        lax.all_gather(ln1_bias, "shard", axis=0, tiled=True),
        lax.all_gather(w_query, "shard", axis=0, tiled=True),
        lax.all_gather(w_key, "shard", axis=0, tiled=True),
        lax.all_gather(w_value, "shard", axis=0, tiled=True),
        lax.all_gather(b_value, "shard", axis=0, tiled=True),
        lax.all_gather(q_gain, "shard", axis=0, tiled=True),
        lax.all_gather(k_gain, "shard", axis=0, tiled=True),
        lax.all_gather(w_out, "shard", axis=0, tiled=True),
        lax.all_gather(b_out, "shard", axis=0, tiled=True),
        lax.all_gather(ln2_gain, "shard", axis=0, tiled=True),
        lax.all_gather(ln2_bias, "shard", axis=0, tiled=True),
        lax.all_gather(w_up, "shard", axis=0, tiled=True),
        lax.all_gather(b_up, "shard", axis=0, tiled=True),
        lax.all_gather(w_down, "shard", axis=0, tiled=True),
        lax.all_gather(b_down, "shard", axis=0, tiled=True),
    )
    f32 = jnp.float32
    ids = image_ids[0]
    allowed = ids[:, None] == ids[None, :]
    x_in = tokens.astype(f32)
    h_one = norm_rows(x_in, full[0].astype(f32), full[1].astype(f32)).astype(jnp.bfloat16)
    q_raw = product(h_one, full[2])
    k_raw = product(h_one, full[3])
    values = (product(h_one, full[4]) + full[5].astype(f32)).astype(jnp.bfloat16)
    query = norm_heads(q_raw, full[6].astype(f32)).astype(jnp.bfloat16)
    key = norm_heads(k_raw, full[7].astype(f32)).astype(jnp.bfloat16)
    q_heads = split_heads(query)
    k_heads = split_heads(key)
    v_heads = split_heads(values)

    def forward_step(carry, items):
        return (carry, head_forward(items[0], items[1], items[2], allowed))

    _, (contexts, logsums) = lax.scan(forward_step, 0, (q_heads, k_heads, v_heads))
    context = merge_heads(contexts)
    x_one = x_in + (product(context, full[8]) + full[9].astype(f32))
    h_two = norm_rows(x_one, full[10].astype(f32), full[11].astype(f32)).astype(jnp.bfloat16)
    pre = product(h_two, full[12]) + full[13].astype(f32)
    act = jax.nn.gelu(pre, approximate=False).astype(jnp.bfloat16)
    outputs = (x_one + (product(act, full[14]) + full[15].astype(f32))).astype(jnp.bfloat16)
    back = (
        lax.all_gather(ln1_gain, "shard", axis=0, tiled=True),
        lax.all_gather(ln1_bias, "shard", axis=0, tiled=True),
        lax.all_gather(w_query, "shard", axis=0, tiled=True),
        lax.all_gather(w_key, "shard", axis=0, tiled=True),
        lax.all_gather(w_value, "shard", axis=0, tiled=True),
        lax.all_gather(b_value, "shard", axis=0, tiled=True),
        lax.all_gather(q_gain, "shard", axis=0, tiled=True),
        lax.all_gather(k_gain, "shard", axis=0, tiled=True),
        lax.all_gather(w_out, "shard", axis=0, tiled=True),
        lax.all_gather(b_out, "shard", axis=0, tiled=True),
        lax.all_gather(ln2_gain, "shard", axis=0, tiled=True),
        lax.all_gather(ln2_bias, "shard", axis=0, tiled=True),
        lax.all_gather(w_up, "shard", axis=0, tiled=True),
        lax.all_gather(b_up, "shard", axis=0, tiled=True),
        lax.all_gather(w_down, "shard", axis=0, tiled=True),
        lax.all_gather(b_down, "shard", axis=0, tiled=True),
    )
    g_b_down = jnp.sum(cotangent.astype(f32), 0)
    g_w_down = contract_rows(act, cotangent)
    d_act = contract_cols(cotangent, back[14])
    _, gelu_pull = jax.vjp(partial(jax.nn.gelu, approximate=False), pre)
    d_pre = gelu_pull(d_act)[0].astype(jnp.bfloat16)
    g_b_up = jnp.sum(d_pre.astype(f32), 0)
    g_w_up = contract_rows(h_two, d_pre)
    d_h_two = contract_cols(d_pre, back[12])
    _, second_pull = jax.vjp(norm_rows, x_one, back[10].astype(f32), back[11].astype(f32))
    d_x_part, g_ln2_gain, g_ln2_bias = second_pull(d_h_two)
    d_x_one = cotangent.astype(f32) + d_x_part
    d_att = d_x_one.astype(jnp.bfloat16)
    g_b_out = jnp.sum(d_att.astype(f32), 0)
    g_w_out = contract_rows(context, d_att)
    d_context = contract_cols(d_att, back[8]).astype(jnp.bfloat16)

    def backward_step(carry, items):
        return (carry, head_backward(items[0], items[1], items[2], items[3], items[4], allowed))

    _, (dq_heads, dk_heads, dv_heads) = lax.scan(
        backward_step, 0, (q_heads, k_heads, v_heads, split_heads(d_context), logsums)
    )
    _, query_pull = jax.vjp(norm_heads, q_raw, back[6].astype(f32))
    d_q_raw, g_q_gain = query_pull(merge_heads(dq_heads))
    _, key_pull = jax.vjp(norm_heads, k_raw, back[7].astype(f32))
    d_k_raw, g_k_gain = key_pull(merge_heads(dk_heads))
    d_q_low = d_q_raw.astype(jnp.bfloat16)
    d_k_low = d_k_raw.astype(jnp.bfloat16)
    d_v_low = merge_heads(dv_heads).astype(jnp.bfloat16)
    g_b_value = jnp.sum(d_v_low.astype(f32), 0)
    g_w_query = contract_rows(h_one, d_q_low)
    g_w_key = contract_rows(h_one, d_k_low)
    g_w_value = contract_rows(h_one, d_v_low)
    d_h_one = (
        contract_cols(d_q_low, back[2])
        + contract_cols(d_k_low, back[3])
        + contract_cols(d_v_low, back[4])
    )
    _, first_pull = jax.vjp(norm_rows, x_in, back[0].astype(f32), back[1].astype(f32))
    d_x_first, g_ln1_gain, g_ln1_bias = first_pull(d_h_one)
    d_tokens = (d_x_one + d_x_first).astype(jnp.bfloat16)
    sg0, sg1, sg2, sg3, sg4, sg5, sg6, sg7, sg8, sg9, sg10, sg11, sg12, sg13, sg14, sg15 = (
        lax.psum_scatter(g_ln1_gain, "shard", scatter_dimension=0, tiled=True),
        lax.psum_scatter(g_ln1_bias, "shard", scatter_dimension=0, tiled=True),
        lax.psum_scatter(g_w_query, "shard", scatter_dimension=0, tiled=True),
        lax.psum_scatter(g_w_key, "shard", scatter_dimension=0, tiled=True),
        lax.psum_scatter(g_w_value, "shard", scatter_dimension=0, tiled=True),
        lax.psum_scatter(g_b_value, "shard", scatter_dimension=0, tiled=True),
        lax.psum_scatter(g_q_gain, "shard", scatter_dimension=0, tiled=True),
        lax.psum_scatter(g_k_gain, "shard", scatter_dimension=0, tiled=True),
        lax.psum_scatter(g_w_out, "shard", scatter_dimension=0, tiled=True),
        lax.psum_scatter(g_b_out, "shard", scatter_dimension=0, tiled=True),
        lax.psum_scatter(g_ln2_gain, "shard", scatter_dimension=0, tiled=True),
        lax.psum_scatter(g_ln2_bias, "shard", scatter_dimension=0, tiled=True),
        lax.psum_scatter(g_w_up, "shard", scatter_dimension=0, tiled=True),
        lax.psum_scatter(g_b_up, "shard", scatter_dimension=0, tiled=True),
        lax.psum_scatter(g_w_down, "shard", scatter_dimension=0, tiled=True),
        lax.psum_scatter(g_b_down, "shard", scatter_dimension=0, tiled=True),
    )
    summed = lax.psum(
        (sg0, sg1, sg2, sg3, sg4, sg5, sg6, sg7, sg8, sg9, sg10, sg11, sg12, sg13, sg14, sg15),
        "rep",
    )
    return (
        outputs,
        d_tokens,
        summed[0],
        summed[1],
        summed[2],
        summed[3],
        summed[4],
        summed[5],
        summed[6],
        summed[7],
        summed[8],
        summed[9],
        summed[10],
        summed[11],
        summed[12],
        summed[13],
        summed[14],
        summed[15],
    )


def solution(mesh):
    return jax.shard_map(
        on_device,
        mesh=mesh,
        in_specs=(
            P(("rep", "shard"), None),
            P(("rep", "shard"), None),
            P("shard"),
            P("shard"),
            P("shard", None),
            P("shard", None),
            P("shard", None),
            P("shard"),
            P("shard"),
            P("shard"),
            P("shard", None),
            P("shard"),
            P("shard"),
            P("shard"),
            P("shard", None),
            P("shard"),
            P("shard", None),
            P("shard"),
            P(("rep", "shard"), None),
        ),
        out_specs=(
            P(("rep", "shard"), None),
            P(("rep", "shard"), None),
            P("shard"),
            P("shard"),
            P("shard", None),
            P("shard", None),
            P("shard", None),
            P("shard"),
            P("shard"),
            P("shard"),
            P("shard", None),
            P("shard"),
            P("shard"),
            P("shard"),
            P("shard", None),
            P("shard"),
            P("shard", None),
            P("shard"),
        ),
        check_vma=False,
    )
```

profile of v0, /device:TPU:0, one launch (start us, length us, event | category | flops | bytes accessed | tf_op | source)
XLA Modules:
  0.0 1099.0 jit_solution(18232146584829334263)
XLA Ops:
  11.3 5.2 all-gather.2
  23.9 4.5 all-gather
  46.0 4.5 all-gather.8
  50.5 4.5 all-gather.7
  89.5 126.9 %while.28 = (s32[]{:T(128)}, bf16[12,1024,64]{1,2,0:T(8,128)(2,1)}, f32[12,1024]{1,0:T(8,128)}, bf16[12,1024,64]{2,1,0:T(8,128)(2,1)}, bf16[12,1024,64]{2,1,0:T(...) while((s32[]{:T(128)}, bf16[12,1024,64]{1,2,0:T(8,128)(2,1)}, ...), condition=%wide.region_9.10_spmd.clone, body=%wide.region_6.9_spmd.clone.sunk | while | flops 284228608 | bytes 30341244 | solution.py:135
  116.7 4.9 fusion.152
  180.0 4.8 fusion.152
  221.9 37.9 %multiply_convert_fusion.1 = (bf16[1024,3072]{1,0:T(8,128)(2,1)}, f32[1024,3072]{1,0:T(8,128)}, f32[1024,3072]{1,0:T(8,128)}) fusion(f32[3072]{0:T(1024)S(1)} %bitcast.232, bf16[768,3072]{1,0:T(8,128)(2,1)} %all-gather.25.cloned.1.call-done, f32[1024,768]{0,1:T(8,128)} %copy-done.11, f32[768]{0:T(1024)S(1)} %reshape.277, f32[768]{0:T(1024)S(1)} %reshape.276, ...), kind=kOutput, calls=%fused_computation.61 | convolution fusion | flops 5043388416 | bytes 39348224 | tf_op jit(solution)/shard_map/dot_general | solution.py:31
  259.8 17.2 %convert_reduce_fusion = (f32[3072]{0:T(1024)S(1)}, bf16[1024,3072]{1,0:T(8,128)(2,1)}) fusion(f32[1024,3072]{1,0:T(8,128)} %get-tuple-element.262, bf16[1024,768]{1,0:T(8,128)(2,1)S(1)} %copy-done.34, bf16[3072,768]{1,0:T(8,128)(2,1)} %all-gather.27.cloned.1.call-done, f32[1024,3072]{1,0:T(8,128)} %get-tuple-element.271, f32[3072]{0:T(1024)S(1)} %bitcast.233), kind=kOutput, calls=%fused_computation.59 | convolution fusion | flops 4885312512 | bytes 37773312 | tf_op jit(solution)/shard_map/dot_general | solution.py:41
  277.0 9.7 fusion.87
  305.3 159.3 %while.29 = (s32[]{:T(128)}, f32[12,1024,64]{1,2,0:T(8,128)}, f32[12,1024,64]{1,2,0:T(8,128)}, bf16[12,1024,64]{1,2,0:T(8,128)(2,1)}, bf16[12,1024,64]{2,1,0:T(8...) while((s32[]{:T(128)}, f32[12,1024,64]{1,2,0:T(8,128)}, ...), condition=%wide.region_16.17_spmd.clone, body=%wide.region_14.16_spmd.clone.sunk | while | flops 681704448 | bytes 34112624 | solution.py:179
  481.0 4.7 fusion.91
  486.0 5.5 fusion.92
  491.6 10.6 fusion.80
  502.3 10.0 fusion.94
  515.8 37.0 %reduce-scatter.9.cloned.1.call-done = f32[384,768]{1,0:T(8,128)} async-done(((f32[768,768]{1,0:T(8,128)}), f32[384,768]{1,0:T(8,128)}) %reduce-scatter.9.cloned.1.call-update) | async-done | bytes 1179664 | tf_op jit(solution)/shard_map/reduce_scatter | solution.py:205
  552.8 36.9 %reduce-scatter.11.cloned.1.call-done = f32[384,768]{1,0:T(8,128)} async-done(((f32[768,768]{1,0:T(8,128)}), f32[384,768]{1,0:T(8,128)}) %reduce-scatter.11.cloned.1.call-update) | async-done | bytes 1179664 | tf_op jit(solution)/shard_map/reduce_scatter | solution.py:206
  589.8 112.9 %reduce-scatter.15.cloned.1.call-done = f32[384,3072]{1,0:T(8,128)} async-done(((f32[768,3072]{1,0:T(8,128)}), f32[384,3072]{1,0:T(8,128)}) %reduce-scatter.15.cloned.1.call-update) | async-done | bytes 4718608 | tf_op jit(solution)/shard_map/reduce_scatter | solution.py:214
  702.6 112.7 %reduce-scatter.17.cloned.1.call-done = f32[1536,768]{1,0:T(8,128)} async-done(((f32[3072,768]{1,0:T(8,128)}), f32[1536,768]{1,0:T(8,128)}) %reduce-scatter.17.cloned.1.call-update) | async-done | bytes 4718608 | tf_op jit(solution)/shard_map/reduce_scatter | solution.py:216
  822.3 4.7 fusion.70
  842.4 8.1 all-reduce.12
  853.8 9.6 add_convert_fusion.4
  866.0 62.4 %all-reduce.10 = (f32[384]{0:T(512)}, f32[384]{0:T(512)}, f32[384]{0:T(512)}, f32[384]{0:T(512)}, f32[384]{0:T(512)}, /*index=5*/f32[384]{0:T(512)}, f32[384]{0:...) all-reduce(f32[384]{0:T(512)S(1)} %dynamic-slice.1, ...), channel_id=1, replica_groups=mesh['rep'=16,'shard'=2] {'rep'}, use_global_device_ids=true, to_apply=%region_25.26 | all-reduce | flops 4992 | bytes 39936 | tf_op jit(solution)/shard_map/psum | solution.py:219
  928.4 153.0 %all-reduce.15.cloned.1.call-done = (f32[384,768]{1,0:T(8,128)}, f32[384,768]{1,0:T(8,128)}, f32[384,768]{1,0:T(8,128)}, f32[384,768]{1,0:T(8,128)}, f32[384,3072]{1,0:T(8,128)}, /*index=5*/f32[1536,768]{1,0:T(8,128)}) async-done(((f32[384,768]{1,0:T(8,128)}, f32[384,768]{1,0:T(8,128)}, f32[384,768]{1,0:T(8,128)}, f32[384,768]{1,0:T(8,128)}, f32[384,3072]{1,0:T(8,128)}, /*index=5*/f32[1536,768]{1,0:T(8,128)}), ...) | async-done | bytes 14155792 | tf_op jit(solution)/shard_map/psum | solution.py:219
  (455 shorter events, 420.6 us)
Async XLA Ops:
  7.2 51.3 %all-gather.19.cloned.1.call-start = ((), (), s32[]{:S(2)}) async-start(), calls=%async_computation.7 | async-start | bytes 1769472 | tf_op jit(solution)/shard_map/all_gather | solution.py:104
  8.0 61.1 %all-gather.17.cloned.1.call-start = ((), (), s32[]{:S(2)}) async-start(), calls=%async_computation.6 | async-start | bytes 1769472 | tf_op jit(solution)/shard_map/all_gather | solution.py:103
  8.7 75.3 %all-gather.21.cloned.1.call-start = ((), (), s32[]{:S(2)}) async-start(), calls=%async_computation.8 | async-start | bytes 1769472 | tf_op jit(solution)/shard_map/all_gather | solution.py:105
  9.4 207.0 %all-gather.23.cloned.1.call-start = ((), (), s32[]{:S(2)}) async-start(), calls=%async_computation.9 | async-start | bytes 1769472 | tf_op jit(solution)/shard_map/all_gather | solution.py:109
  10.0 211.9 %all-gather.25.cloned.1.call-start = ((), (), s32[]{:S(2)}) async-start(), calls=%async_computation.10 | async-start | bytes 7077888 | tf_op jit(solution)/shard_map/all_gather | solution.py:113
  10.6 249.2 %all-gather.27.cloned.1.call-start = ((), (), s32[]{:S(2)}) async-start(), calls=%async_computation.11 | async-start | bytes 7077888 | tf_op jit(solution)/shard_map/all_gather | solution.py:115
  11.2 501.1 %reduce-scatter.13.cloned.1.call-start = ((), (), s32[]{:S(2)}) async-start(), calls=%async_computation.15 | async-start | bytes 3538944 | tf_op jit(solution)/shard_map/reduce_scatter | solution.py:210
  22.3 28.2 %copy-start.63 = (bf16[384]{0:T(512)(128)(2,1)S(1)}, bf16[384]{0:T(512)(128)(2,1)}, u32[]{:S(2)}) copy-start(bf16[384]{0:T(512)(128)(2,1)} %param.36) | copy-start | bytes 2308
  23.1 33.6 %copy-start.6 = (bf16[1024,768]{0,1:T(8,128)(2,1)}, bf16[1024,768]{0,1:T(8,128)(2,1)S(1)}, u32[]{:S(2)}) copy-start(bf16[1024,768]{0,1:T(8,128)(2,1)S(1)} %copy.51) | copy-start | bytes 4718596
  23.1 32.0 %copy-start.33 = (bf16[1024,768]{1,0:T(8,128)(2,1)S(1)}, bf16[1024,768]{1,0:T(8,128)(2,1)}, u32[]{:S(2)}) copy-start(bf16[1024,768]{1,0:T(8,128)(2,1)} %param.41) | copy-start | bytes 4718596
  23.4 35.1 %copy-start.45 = (f32[1024]{0:T(1024)}, f32[1024]{0:T(1024)S(1)}, u32[]{:S(2)}) copy-start(f32[1024]{0:T(1024)S(1)} %broadcast_multiply_fusion.3) | copy-start | bytes 12292
  23.9 34.6 %copy-start.51 = (f32[1024]{0:T(1024)}, f32[1024]{0:T(1024)S(1)}, u32[]{:S(2)}) copy-start(f32[1024]{0:T(1024)S(1)} %fusion.78) | copy-start | bytes 12292
  28.4 30.0 %copy-start.49 = (f32[768]{0:T(1024)}, f32[768]{0:T(1024)S(1)}, u32[]{:S(2)}) copy-start(f32[768]{0:T(1024)S(1)} %reshape.270) | copy-start | bytes 9220
  89.5 126.9 %copy-start.7 = (bf16[1024,768]{0,1:T(8,128)(2,1)S(1)}, bf16[1024,768]{0,1:T(8,128)(2,1)}, u32[]{:S(2)}) copy-start(bf16[1024,768]{0,1:T(8,128)(2,1)} %copy-done.6) | copy-start | bytes 4718596
  221.9 37.9 %copy-start.34 = (bf16[1024,768]{1,0:T(8,128)(2,1)S(1)}, bf16[1024,768]{1,0:T(8,128)(2,1)}, u32[]{:S(2)}) copy-start(bf16[1024,768]{1,0:T(8,128)(2,1)} %param.41) | copy-start | bytes 4718596
  299.6 216.2 %reduce-scatter.7.cloned.1.call-start = ((), (), s32[]{:S(2)}) async-start(), calls=%async_computation.12 | async-start | bytes 3538944 | tf_op jit(solution)/shard_map/reduce_scatter | solution.py:204
  305.3 159.4 %copy-start.3 = (f32[1024,768]{0,1:T(8,128)S(1)}, f32[1024,768]{0,1:T(8,128)}, u32[]{:S(2)}) copy-start(f32[1024,768]{0,1:T(8,128)} %copy-done.2) | copy-start | bytes 9437188
  305.3 159.4 %copy-start.23 = (f32[1024,12]{0,1:T(8,128)S(1)}, f32[1024,12]{0,1:T(8,128)}, u32[]{:S(2)}) copy-start(f32[1024,12]{0,1:T(8,128)} %copy-done.22) | copy-start | bytes 147460
  305.3 159.4 %copy-start.47 = (f32[12,64]{1,0:T(8,128)S(1)}, f32[12,64]{1,0:T(8,128)}, u32[]{:S(2)}) copy-start(f32[12,64]{1,0:T(8,128)} %mul.336) | copy-start | bytes 9220
  481.0 71.9 %reduce-scatter.9.cloned.1.call-start = ((), (), s32[]{:S(2)}) async-start(), calls=%async_computation.13 | async-start | bytes 3538944 | tf_op jit(solution)/shard_map/reduce_scatter | solution.py:205
  485.7 104.0 %reduce-scatter.11.cloned.1.call-start = ((), (), s32[]{:S(2)}) async-start(), calls=%async_computation.14 | async-start | bytes 3538944 | tf_op jit(solution)/shard_map/reduce_scatter | solution.py:206
  491.5 211.1 %reduce-scatter.15.cloned.1.call-start = ((), (), s32[]{:S(2)}) async-start(), calls=%async_computation.16 | async-start | bytes 14155776 | tf_op jit(solution)/shard_map/reduce_scatter | solution.py:214
  502.2 313.2 %reduce-scatter.17.cloned.1.call-start = ((), (), s32[]{:S(2)}) async-start(), calls=%async_computation.17 | async-start | bytes 14155776 | tf_op jit(solution)/shard_map/reduce_scatter | solution.py:216
  512.2 569.2 %all-reduce.15.cloned.1.call-start = ((), (), s32[]{:S(2)}) async-start(), calls=%async_computation.18 | async-start | bytes 28311552 | tf_op jit(solution)/shard_map/psum | solution.py:219
  (70 other events, 264.3 us)
Sparse Core Ops, SparseCore 0:
  9.6 25.5 all-gather.18
  36.7 22.8 all-gather.16
  61.2 22.7 all-gather.20
  85.4 22.7 all-gather.22
  109.6 62.6 all-gather.24
  173.7 62.6 all-gather.26
  299.8 34.7 reduce-scatter.12
  481.1 34.6 reduce-scatter.6
  518.1 34.7 reduce-scatter.8
  555.0 34.6 reduce-scatter.10
  592.1 110.5 reduce-scatter.14
  704.8 110.5 reduce-scatter.16
  820.5 260.8 all-reduce.14
where the time goes:
time: 1110 us; the launch traced here: 1100 us
  waiting for transfers between devices  464 us (42%)
  matrix products  343 us (31%)
  blocking collectives  115 us (10%)
  local copies, waits for them, and re-layouts  99.9 us (9%)
  other arithmetic  58.9 us (5%)
  between operations  16.4 us (1%)
    psum x1, waiting for transfers between devices, on_device(): lax.psum((sg0, sg1, sg2, sg3, sg4, sg5, sg6, sg7, sg8, sg9, sg10, sg11, s...  153 us
    dot_general x30, matrix products, product(): return jnp.dot(left, right, preferred_element_type=jnp.float32)  138 us
    reduce_scatter x1, waiting for transfers between devices, on_device(): lax.psum_scatter(g_w_up, 'shard', scatter_dimension=0, tiled=True)  113 us
    reduce_scatter x1, waiting for transfers between devices, on_device(): lax.psum_scatter(g_w_down, 'shard', scatter_dimension=0, tiled=True)  113 us
    dot_general x42, matrix products, contract_cols(): lax.dot_general(left, right, (((1,), (1,)), ((), ())), preferred_element_...  111 us
    dot_general x30, matrix products, contract_rows(): lax.dot_general(left, right, (((0,), (0,)), ((), ())), preferred_element_...  94 us
    psum x1, blocking collectives, on_device(): lax.psum((sg0, sg1, sg2, sg3, sg4, sg5, sg6, sg7, sg8, sg9, sg10, sg11, s...  62.4 us
    reduce_scatter x1, waiting for transfers between devices, on_device(): lax.psum_scatter(g_w_key, 'shard', scatter_dimension=0, tiled=True)  37 us
  transfers between devices with their start and end apart: 13, of which 7 were waited for; matrix products, arithmetic and copies ran while one was open for 38% of the time, Pallas kernels for 0%

commit v1 on v0

v1 whole, which is shorter than its diff:
```python
import functools
import math

import jax
import jax.numpy as jnp
from jax import lax
from jax.experimental import pallas as pl
from jax.experimental.pallas import tpu as pltpu
from jax.sharding import PartitionSpec as P

T = 1024
D = 768
FF = 3072
HEADS = 12
DH = D // HEADS
EPS = 1e-06
SCALE = 1.0 / math.sqrt(DH)
RSQRT2 = math.sqrt(0.5)
RSQRT2PI = 1.0 / math.sqrt(2.0 * math.pi)

HD = D // 2
HF = FF // 2
NJ = 6
FC = FF // NJ
FH = FC // 2
RB = 256
NR = T // RB
KB = 256
NK = T // KB

VEC = dict(
    ln1_gain=0,
    ln1_bias=1 * HD,
    b_value=2 * HD,
    q_gain=3 * HD,
    k_gain=4 * HD,
    b_out=5 * HD,
    ln2_gain=6 * HD,
    ln2_bias=7 * HD,
    b_down=8 * HD,
    b_up=9 * HD,
)
NV = 9 * HD + HF

f32 = jnp.float32
bf16 = jnp.bfloat16
MESH = pl.DeviceIdType.MESH


def dot(left, right, cl, cr):
    return lax.dot_general(left, right, (((cl,), (cr,)), ((), ())), preferred_element_type=f32)


def rows_loop(body):
    def step(r, carry):
        body(pl.ds(pl.multiple_of(r * RB, RB), RB))
        return carry

    lax.fori_loop(0, NR, step, 0)


def head_mean(value, avg):
    high = value.astype(bf16)
    low = (value - high.astype(f32)).astype(bf16)
    return dot(high, avg, 1, 0) + dot(low, avg, 1, 0)


def row_stats(value):
    centre = value - jnp.mean(value, -1, keepdims=True)
    spread = jnp.mean(centre * centre, -1, keepdims=True)
    inv = lax.rsqrt(spread + EPS)
    return centre * inv, inv


def vector(vec, name):
    at = VEC[name]
    return jnp.concatenate([vec[0, :, at : at + HD], vec[1, :, at : at + HD]], 1)


def add_vector(gvec, name, total):
    at = VEC[name]
    gvec[0, :, at : at + HD] += total[:, :HD]
    gvec[1, :, at : at + HD] += total[:, HD:]


def col_sum(value):
    return jnp.sum(value, 0, keepdims=True)


class Plain:
    def __init__(self, ins, outs, refs):
        self.ins, self.outs, self.refs = ins, outs, refs

    def begin(self):
        i, r, sem = self.ins, self.refs, self.refs["load_sem"]
        pairs = [(i[n], r["w4"].at[k]) for k, n in enumerate(("w_query", "w_key", "w_value", "w_out"))]
        for j in range(NJ):
            for h in range(2):
                pairs.append((i["w_up"].at[:, pl.ds(h * HF + j * FH, FH)], r["wup"].at[j, :, pl.ds(h * FH, FH)]))
                pairs.append((i["w_down"].at[pl.ds(h * HF + j * FH, FH), :], r["wdn"].at[j, pl.ds(h * FH, FH), :]))
        pairs.append((i["vec"], r["vec"]))
        copies = [pltpu.make_async_copy(a, b, sem.at[k]) for k, (a, b) in enumerate(pairs)]
        for c in copies:
            c.start()
        for c in copies:
            c.wait()

    def weights(self, point, j=None):
        pass

    def put(self, pairs):
        copies = [pltpu.make_async_copy(a, b, self.refs["load_sem"].at[k]) for k, (a, b) in enumerate(pairs)]
        for c in copies:
            c.start()
        for c in copies:
            c.wait()

    def emit_mlp(self, j, up, down):
        gu, gd, o = self.refs["g_up"], self.refs["g_dn"], self.outs
        gu[0] = up()
        gd[0] = down()
        pairs = []
        for h in range(2):
            at = pl.multiple_of(h * HF + j * FH, FH)
            pairs.append((gu.at[0, :, pl.ds(h * FH, FH)], o["g_up"].at[:, pl.ds(at, FH)]))
            pairs.append((gd.at[0, pl.ds(h * FH, FH), :], o["g_down"].at[pl.ds(at, FH), :]))
        self.put(pairs)

    def emit_out(self, value):
        self.refs["g_sq"][0] = value()
        self.put([(self.refs["g_sq"].at[0], self.outs["g_out"])])

    def emit_qkv(self, g, value):
        gs = self.refs["g_sq"]
        gs[0] = value()
        pairs = []
        for c in range(2):
            for k in range(3):
                pairs.append(
                    (gs.at[0, :, pl.ds((c * 3 + k) * 128, 128)], self.outs["g_qkv"].at[k, :, pl.ds((2 * g + c) * 128, 128)])
                )
        self.put(pairs)

    def slot(self, name, j=None):
        pass

    def finish(self):
        self.put([(self.refs["gvec"], self.outs["gvec"])])


def compute(comm, ins, outs, refs):
    r = refs
    h1, qs, ks, vs, ctx = r["h1"], r["qs"], r["ks"], r["vs"], r["ctx"]
    vec, gvec, w4, wup, wdn = r["vec"], r["gvec"], r["w4"], r["wup"], r["wdn"]
    tok, cot, h2, x1, yacc, dh2 = r["tok"], r["cot"], r["h2"], r["x1"], r["yacc"], r["dh2"]
    sem = r["io_sem"]

    load_tok = pltpu.make_async_copy(ins["tokens"], tok, sem.at[0])
    load_ids = pltpu.make_async_copy(ins["ids"], r["idr"], sem.at[1])
    load_cot = pltpu.make_async_copy(ins["cotangent"], cot, sem.at[2])
    load_tok.start()
    load_ids.start()
    comm.begin()
    load_cot.start()
    gvec[...] = jnp.zeros_like(gvec)
    pair = lax.broadcasted_iota(jnp.int32, (256, 256), 0) // DH
    same = pair == lax.broadcasted_iota(jnp.int32, (256, 256), 1) // DH
    r["avg"][...] = jnp.where(same, 1.0 / DH, 0.0).astype(bf16)
    load_ids.wait()
    r["idc"][...] = jnp.broadcast_to(r["idr"][...], (128, T)).T
    load_tok.wait()
    load_cot.wait()

    comm.weights("vec")

    def ln1(rows):
        hat, _ = row_stats(tok[rows, :].astype(f32))
        h1[rows, :] = (hat * vector(vec, "ln1_gain") + vector(vec, "ln1_bias")).astype(bf16)
        add_vector(gvec, "b_down", col_sum(cot[rows, :].astype(f32)))

    rows_loop(ln1)

    for k, (name, raw, low) in enumerate((("q_gain", yacc, qs), ("k_gain", dh2, ks))):
        comm.weights("w4", k)

        def project(rows):
            value = dot(h1[rows, :], w4[k], 1, 0)
            raw[rows, :] = value
            gain = vector(vec, name)
            for b in range(D // 256):
                cols = slice(b * 256, (b + 1) * 256)
                centre = value[:, cols] - head_mean(value[:, cols], r["avg"][...])
                spread = head_mean(centre * centre, r["avg"][...])
                low[rows, cols] = (centre * lax.rsqrt(spread + EPS) * gain[:, cols]).astype(bf16)

        rows_loop(project)
    comm.weights("w4", 2)

    def project_values(rows):
        vs[rows, :] = (dot(h1[rows, :], w4[2], 1, 0) + vector(vec, "b_value")).astype(bf16)

    rows_loop(project_values)
    save = [
        pltpu.make_async_copy(yacc, outs["q_raw"], sem.at[3]),
        pltpu.make_async_copy(dh2, outs["k_raw"], sem.at[4]),
    ]
    for c in save:
        c.start()

    lane = lax.broadcasted_iota(jnp.int32, (1, 128), 1)
    first = lane < DH
    halves = (first, jnp.logical_not(first))
    oacc = r["oacc"]
    ones = jnp.ones((KB, 128), bf16)

    def attend(hp, carry):
        cols = pl.ds(pl.multiple_of(hp * 128, 128), 128)
        oacc[...] = jnp.zeros_like(oacc)
        for j in range(NK):
            lo, hi = max(0, j - 1) * KB, min(NK, j + 2) * KB
            key = ks[j * KB : (j + 1) * KB, cols]
            wide = jnp.concatenate([vs[j * KB : (j + 1) * KB, cols], ones], 1)
            query = qs[lo:hi, cols]
            allowed = r["idc"][lo:hi, 0:1] == r["idr"][:, j * KB : (j + 1) * KB]
            for h in range(2):
                scores = dot(query, jnp.where(halves[h], key, jnp.zeros_like(key)), 1, 1)
                probs = jnp.where(allowed, jnp.exp(scores * SCALE), 0.0).astype(bf16)
                oacc[h, lo:hi, :] += dot(probs, wide, 1, 0)
        inv0 = 1.0 / oacc[0, :, 128:]
        inv1 = 1.0 / oacc[1, :, 128:]
        ctx[:, cols] = jnp.where(first, oacc[0, :, :128] * inv0, oacc[1, :, :128] * inv1).astype(bf16)
        r["inv"][hp] = jnp.where(first, inv0, inv1)
        comm.weights("attend", hp)
        return carry

    lax.fori_loop(0, HEADS // 2, attend, 0)
    for c in save:
        c.wait()

    comm.weights("w4", 3)

    def out_rows(rows):
        value = tok[rows, :].astype(f32) + (dot(ctx[rows, :], w4[3], 1, 0) + vector(vec, "b_out"))
        x1[rows, :] = value
        yacc[rows, :] = value + vector(vec, "b_down")
        dh2[rows, :] = jnp.zeros((RB, D), f32)
        hat, _ = row_stats(value)
        h2[rows, :] = (hat * vector(vec, "ln2_gain") + vector(vec, "ln2_bias")).astype(bf16)

    rows_loop(out_rows)

    act, dpre = r["act"], r["dpre"]

    def chunk(j, carry):
        comm.weights("mlp", j)
        at = pl.multiple_of(VEC["b_up"] + j * FH, 128)
        bias = jnp.concatenate([vec[0, :, pl.ds(at, FH)], vec[1, :, pl.ds(at, FH)]], 1)

        def mlp_rows(rows):
            pre = dot(h2[rows, :], wup[j], 1, 0) + bias
            d_act = dot(cot[rows, :], wdn[j], 1, 1)
            cdf = 0.5 * (1.0 + lax.erf(pre * RSQRT2))
            pdf = jnp.exp(-0.5 * pre * pre) * RSQRT2PI
            low = (pre * cdf).astype(bf16)
            d_low = (d_act * (cdf + pre * pdf)).astype(bf16)
            act[rows, :] = low
            dpre[rows, :] = d_low
            total = col_sum(d_low.astype(f32))
            gvec[0, :, pl.ds(at, FH)] += total[:, :FH]
            gvec[1, :, pl.ds(at, FH)] += total[:, FH:]
            yacc[rows, :] += dot(low, wdn[j], 1, 0)
            dh2[rows, :] += dot(d_low, wup[j], 1, 1)

        rows_loop(mlp_rows)
        comm.slot("mlp", j)
        comm.emit_mlp(
            j,
            lambda: dot(h2[...], dpre[...], 0, 0).astype(bf16),
            lambda: dot(act[...], cot[...], 0, 0).astype(bf16),
        )
        return carry

    lax.fori_loop(0, NJ, chunk, 0)

    low_out = r["low_out"]

    def ln2_back(rows):
        low_out[rows, :] = yacc[rows, :].astype(bf16)
        hat, inv = row_stats(x1[rows, :])
        d_h2 = dh2[rows, :]
        add_vector(gvec, "ln2_gain", col_sum(d_h2 * hat))
        add_vector(gvec, "ln2_bias", col_sum(d_h2))
        scaled = d_h2 * vector(vec, "ln2_gain")
        mean = jnp.mean(scaled, -1, keepdims=True)
        along = jnp.mean(scaled * hat, -1, keepdims=True)
        d_x1 = cot[rows, :].astype(f32) + inv * (scaled - mean - hat * along)
        dh2[rows, :] = d_x1
        d_att = d_x1.astype(bf16)
        h2[rows, :] = d_att
        add_vector(gvec, "b_out", col_sum(d_att.astype(f32)))
        cot[rows, :] = dot(d_att, w4[3], 1, 1).astype(bf16)

    rows_loop(ln2_back)
    store_out = pltpu.make_async_copy(low_out, outs["outputs"], sem.at[5])
    store_out.start()
    comm.slot("ln2")
    comm.emit_out(lambda: dot(ctx[...], h2[...], 0, 0).astype(bf16))
    comm.slot("out")

    d_h1 = x1
    raw_q, raw_k, dqf, dkf, dql = r["raw_q"], r["raw_k"], r["dqf"], r["dkf"], r["dql"]
    for g in range(HEADS // 4):
        gcols = slice(g * 256, (g + 1) * 256)
        back = [
            pltpu.make_async_copy(outs["q_raw"].at[:, pl.ds(g * 256, 256)], raw_q, sem.at[6]),
            pltpu.make_async_copy(outs["k_raw"].at[:, pl.ds(g * 256, 256)], raw_k, sem.at[7]),
        ]
        for c in back:
            c.start()

        def attend_back(p, carry):
            hp = 2 * g + p
            cols = pl.ds(pl.multiple_of(hp * 128, 128), 128)
            local = pl.ds(pl.multiple_of(p * 128, 128), 128)
            vcols = pl.ds(pl.multiple_of(p * 384 + 256, 128), 128)
            product = cot[:, cols].astype(f32) * ctx[:, cols].astype(f32)
            deltas = [jnp.sum(jnp.where(m, product, 0.0), -1, keepdims=True) for m in halves]
            inv = r["inv"][hp]
            invs = (inv[:, 0:1], inv[:, DH : DH + 1])
            dqf[:, local] = jnp.zeros((T, 128), f32)
            for j in range(NK):
                lo, hi = max(0, j - 1) * KB, min(NK, j + 2) * KB
                tile = slice(j * KB, (j + 1) * KB)
                key, value = ks[tile, cols], vs[tile, cols]
                query, d_ctx = qs[lo:hi, cols], cot[lo:hi, cols]
                allowed = r["idc"][lo:hi, 0:1] == r["idr"][:, tile]
                d_keys, d_values = [], []
                for h in range(2):
                    key_h = jnp.where(halves[h], key, jnp.zeros_like(key))
                    value_h = jnp.where(halves[h], value, jnp.zeros_like(value))
                    scores = dot(query, key_h, 1, 1)
                    probs = jnp.where(allowed, jnp.exp(scores * SCALE) * invs[h][lo:hi], 0.0)
                    d_probs = dot(d_ctx, value_h, 1, 1)
                    d_scores = (probs * (d_probs - deltas[h][lo:hi])).astype(bf16)
                    dqf[lo:hi, local] += dot(d_scores, key_h, 1, 0)
                    d_values.append(dot(probs.astype(bf16), d_ctx, 0, 0))
                    d_keys.append(dot(d_scores, query, 0, 0))
                dkf[tile, local] = jnp.where(first, d_keys[0], d_keys[1])
                dql[tile, vcols] = jnp.where(first, d_values[0], d_values[1]).astype(bf16)
            return carry

        lax.fori_loop(0, 2, attend_back, 0)
        comm.slot("att", g)
        for c in back:
            c.wait()

        def heads_back(rows):
            for k, (name, raw, grad) in enumerate((("q_gain", raw_q, dqf), ("k_gain", raw_k, dkf))):
                value = raw[rows, :]
                centre = value - head_mean(value, r["avg"][...])
                inv = lax.rsqrt(head_mean(centre * centre, r["avg"][...]) + EPS)
                hat = centre * inv
                d_low = grad[rows, :] * SCALE
                total = col_sum(d_low * hat)
                gain = vector(vec, name)[:, gcols]
                scaled = d_low * gain
                mean = head_mean(scaled, r["avg"][...])
                along = head_mean(scaled * hat, r["avg"][...])
                d_raw = (inv * (scaled - mean - hat * along)).astype(bf16)
                for c in range(2):
                    dql[rows, (c * 3 + k) * 128 : (c * 3 + k + 1) * 128] = d_raw[:, c * 128 : (c + 1) * 128]
                add_group(gvec, name, g, total)
            d_value = jnp.concatenate([dql[rows, 256:384], dql[rows, 640:768]], 1).astype(f32)
            add_group(gvec, "b_value", g, col_sum(d_value))

        rows_loop(heads_back)
        comm.emit_qkv(g, lambda: dot(h1[...], dql[...], 0, 0).astype(bf16))

        def h1_back(rows):
            total = None
            for k in range(3):
                d_low = jnp.concatenate([dql[rows, (c * 3 + k) * 128 : (c * 3 + k + 1) * 128] for c in range(2)], 1)
                part = dot(d_low, w4[k, :, gcols], 1, 1)
                total = part if total is None else total + part
            if g == 0:
                d_h1[rows, :] = total
            else:
                d_h1[rows, :] += total

        if g == 0:
            store_out.wait()
            again = pltpu.make_async_copy(ins["tokens"], tok, sem.at[0])
            again.start()
        rows_loop(h1_back)
        comm.slot("qkv", g)

    again.wait()

    def ln1_back(rows):
        hat, inv = row_stats(tok[rows, :].astype(f32))
        grad = d_h1[rows, :]
        add_vector(gvec, "ln1_gain", col_sum(grad * hat))
        add_vector(gvec, "ln1_bias", col_sum(grad))
        scaled = grad * vector(vec, "ln1_gain")
        mean = jnp.mean(scaled, -1, keepdims=True)
        along = jnp.mean(scaled * hat, -1, keepdims=True)
        low_out[rows, :] = (dh2[rows, :] + inv * (scaled - mean - hat * along)).astype(bf16)

    rows_loop(ln1_back)
    store_tok = pltpu.make_async_copy(low_out, outs["d_tokens"], sem.at[5])
    store_tok.start()
    comm.finish()
    store_tok.wait()


def add_group(gvec, name, g, total):
    for c in range(2):
        col = g * 256 + c * 128
        at = VEC[name] + col % HD
        gvec[col // HD, :, at : at + 128] += total[:, c * 128 : (c + 1) * 128]


def scratch_common():
    vm = pltpu.VMEM
    return dict(
        w4=vm((4, D, D), bf16),
        wup=vm((NJ, D, FC), bf16),
        wdn=vm((NJ, FC, D), bf16),
        vec=vm((2, 1, NV), f32),
        gvec=vm((2, 1, NV), f32),
        avg=vm((256, 256), bf16),
        idr=vm((1, T), jnp.int32),
        idc=vm((T, 128), jnp.int32),
        tok=vm((T, D), bf16),
        cot=vm((T, D), bf16),
        h1=vm((T, D), bf16),
        qs=vm((T, D), bf16),
        ks=vm((T, D), bf16),
        vs=vm((T, D), bf16),
        ctx=vm((T, D), bf16),
        inv=vm((HEADS // 2, T, 128), f32),
        x1=vm((T, D), f32),
        h2=vm((T, D), bf16),
        yacc=vm((T, D), f32),
        dh2=vm((T, D), f32),
        low_out=vm((T, D), bf16),
        act=vm((T, FC), bf16),
        dpre=vm((T, FC), bf16),
        oacc=vm((2, T, 256), f32),
        raw_q=vm((T, 256), f32),
        raw_k=vm((T, 256), f32),
        dqf=vm((T, 256), f32),
        dkf=vm((T, 256), f32),
        dql=vm((T, D), bf16),
        io_sem=pltpu.SemaphoreType.DMA((8,)),
    )


def scratch_plain():
    vm = pltpu.VMEM
    return dict(
        scratch_common(),
        g_up=vm((1, D, FC), bf16),
        g_dn=vm((1, FC, D), bf16),
        g_sq=vm((1, D, D), bf16),
        load_sem=pltpu.SemaphoreType.DMA((32,)),
    )


IN_NAMES = ("tokens", "ids", "cotangent", "w_query", "w_key", "w_value", "w_out", "w_up", "w_down", "vec")


def run_kernel(make_comm, out_shapes, scratch, args, params):
    out_names, scratch_names = tuple(out_shapes), tuple(scratch)

    def kernel(*all_refs):
        n_in, n_out = len(IN_NAMES), len(out_names)
        ins = dict(zip(IN_NAMES, all_refs[:n_in]))
        outs = dict(zip(out_names, all_refs[n_in : n_in + n_out]))
        refs = dict(zip(scratch_names, all_refs[n_in + n_out :]))
        compute(make_comm(ins, outs, refs), ins, outs, refs)

    anywhere = pl.BlockSpec(memory_space=pl.ANY)
    result = pl.pallas_call(
        kernel,
        out_shape=tuple(out_shapes.values()),
        in_specs=[anywhere] * len(IN_NAMES),
        out_specs=(anywhere,) * len(out_names),
        scratch_shapes=list(scratch.values()),
        compiler_params=params,
        name="encoder_layer",
    )(*[args[n] for n in IN_NAMES])
    return dict(zip(out_names, result))


def shape(dims, dtype):
    return jax.ShapeDtypeStruct(dims, dtype)


VECTORS = ("ln1_gain", "ln1_bias", "b_value", "q_gain", "k_gain", "b_out", "ln2_gain", "ln2_bias", "b_down", "b_up")


def plain_layer(a):
    def whole(value):
        return lax.all_gather(value, "shard", axis=0, tiled=True)

    args = dict(tokens=a["tokens"], ids=a["image_ids"], cotangent=a["cotangent"])
    for n in ("w_query", "w_key", "w_value", "w_out", "w_up", "w_down"):
        args[n] = whole(a[n])
    vecs = [whole(a[n]).astype(f32).reshape(2, -1) for n in VECTORS]
    args["vec"] = jnp.concatenate(vecs, 1).reshape(2, 1, NV)
    out_shapes = dict(
        outputs=shape((T, D), bf16),
        d_tokens=shape((T, D), bf16),
        g_up=shape((D, FF), bf16),
        g_down=shape((FF, D), bf16),
        g_out=shape((D, D), bf16),
        g_qkv=shape((3, D, D), bf16),
        gvec=shape((2, 1, NV), f32),
        q_raw=shape((T, D), f32),
        k_raw=shape((T, D), f32),
    )
    params = pltpu.CompilerParams(vmem_limit_bytes=67043328)
    o = run_kernel(Plain, out_shapes, scratch_plain(), args, params)

    def reduce(value):
        part = lax.psum_scatter(value.astype(f32), "shard", scatter_dimension=0, tiled=True)
        return lax.psum(part, "rep")

    grads = dict(w_out=o["g_out"], w_up=o["g_up"], w_down=o["g_down"])
    for k, n in enumerate(("w_query", "w_key", "w_value")):
        grads[n] = o["g_qkv"][k]
    gvec = o["gvec"].reshape(2, NV)
    for n in VECTORS:
        at = VEC[n]
        size = HF if n == "b_up" else HD
        grads[n] = gvec[:, at : at + size].reshape(-1)
    grads = {n: reduce(v) for n, v in grads.items()}
    return o["outputs"], o["d_tokens"], grads


ARGS = (
    "tokens",
    "image_ids",
    "ln1_gain",
    "ln1_bias",
    "w_query",
    "w_key",
    "w_value",
    "b_value",
    "q_gain",
    "k_gain",
    "w_out",
    "b_out",
    "ln2_gain",
    "ln2_bias",
    "w_up",
    "b_up",
    "w_down",
    "b_down",
    "cotangent",
)


def specs(names):
    both = P(("rep", "shard"), None)
    table = dict(tokens=both, image_ids=both, cotangent=both)
    return tuple(table.get(n, P("shard", None) if n.startswith("w_") else P("shard")) for n in names)


def solution(mesh):
    def on_device(*values):
        outputs, d_tokens, grads = plain_layer(dict(zip(ARGS, values)))
        return (outputs, d_tokens) + tuple(grads[n] for n in ARGS[2:-1])

    both = P(("rep", "shard"), None)
    return jax.shard_map(
        on_device,
        mesh=mesh,
        in_specs=specs(ARGS),
        out_specs=(both, both) + specs(ARGS[2:-1]),
        check_vma=False,
    )
```

time: 1110 us -> 1060 us (0.955)
  matrix products: 343 us -> 0 us
  waiting for transfers between devices: 464 us -> 731 us
  Pallas kernels: 0 us -> 152 us
  local copies, waits for them, and re-layouts: 99.9 us -> 13.7 us
  other arithmetic: 58.9 us -> 20.6 us
    dot_general x102 -> x0, matrix products: 343 us -> none  [the longest x30 138 us: product(): return jnp.dot(left, right, preferred_element_type=jnp.float32)]
    all_gather x6, waiting for transfers between devices: 4.22 us -> 180 us  [whole(): return lax.all_gather(value, 'shard', axis=0, tiled=True)]
    pallas_call x0 -> x1, Pallas kernels: none -> 152 us  [run_kernel(): pl.pallas_call(kernel, out_shape=tuple(out_shapes.values()), in_specs=[an...]
    reduce_scatter x6, waiting for transfers between devices: 303 us -> 354 us  [reduce(): lax.psum_scatter(value.astype(f32), 'shard', scatter_dimension=0, tiled=T...]
    psum x1, waiting for transfers between devices: 153 us -> 192 us  [reduce(): return lax.psum(part, 'rep')]
    reduce_sum x30 -> x0, other arithmetic: 36.8 us -> none  [the longest x12 12.4 us: head_forward(): total = jnp.sum(expo, -1, keepdims=True)]
    while x24 -> x0, local copies, waits for them, and re-layouts: 24.1 us -> none
    unnamed x169 -> x75, local copies, waits for them, and re-layouts: 30.5 us -> 13 us
  transfers between devices with their start and end apart: 13 -> 13, of which waited for: 7 -> 12; matrix products, arithmetic and copies ran while one was open for 38% -> 2% of each run, Pallas kernels for 0% -> 0%
where the time goes in v1:
time: 1060 us; the launch traced here: 1050 us
  waiting for transfers between devices  731 us (69%)
  Pallas kernels  152 us (14%)
  blocking collectives  115 us (11%)
  other arithmetic  20.6 us (2%)
  between operations  15.8 us (1%)
  local copies, waits for them, and re-layouts  13.7 us (1%)
    reduce_scatter x6, waiting for transfers between devices, reduce(): lax.psum_scatter(value.astype(f32), 'shard', scatter_dimension=0, tiled=T...  354 us
    psum x1, waiting for transfers between devices, reduce(): return lax.psum(part, 'rep')  192 us
    all_gather x6, waiting for transfers between devices, whole(): return lax.all_gather(value, 'shard', axis=0, tiled=True)  180 us
    pallas_call x1, Pallas kernels, run_kernel(): pl.pallas_call(kernel, out_shape=tuple(out_shapes.values()), in_specs=[an...  152 us
    psum x1, blocking collectives, reduce(): return lax.psum(part, 'rep')  62.9 us
    all_gather x10, blocking collectives, whole(): return lax.all_gather(value, 'shard', axis=0, tiled=True)  44.3 us
  transfers between devices with their start and end apart: 13, of which 12 were waited for; matrix products, arithmetic and copies ran while one was open for 2% of the time, Pallas kernels for 0%

profile of v1, /device:TPU:0, one launch (start us, length us, event | category | flops | bytes accessed | tf_op | source)
XLA Modules:
  0.0 1048.3 jit_solution(4287142659252549723)
XLA Ops:
  11.5 5.2 all-gather
  21.1 4.3 all-gather.2
  25.4 4.3 all-gather.3
  29.7 4.3 all-gather.4
  42.7 4.3 all-gather.7
  47.0 4.3 all-gather.8
  51.4 4.5 all-gather.9
  59.6 24.4 %all-gather.21.cloned.1.call-done.all_refs_5_ = bf16[768,768]{1,0:T(8,128)(2,1)} async-done(((bf16[384,768]{1,0:T(8,128)(2,1)}), bf16[768,768]{1,0:T(8,128)(2,1)}) %all-gather.21.cloned.1.call-update) | async-done | bytes 1179664 | tf_op jit(solution)/shard_map/all_gather | solution.py:505
  84.1 24.2 %all-gather.23.cloned.1.call-done.all_refs_6_ = bf16[768,768]{1,0:T(8,128)(2,1)} async-done(((bf16[384,768]{1,0:T(8,128)(2,1)}), bf16[768,768]{1,0:T(8,128)(2,1)}) %all-gather.23.cloned.1.call-update) | async-done | bytes 1179664 | tf_op jit(solution)/shard_map/all_gather | solution.py:505
  108.3 64.1 %all-gather.25.cloned.1.call-done.all_refs_7_ = bf16[768,3072]{1,0:T(8,128)(2,1)} async-done(((bf16[384,3072]{1,0:T(8,128)(2,1)}), bf16[768,3072]{1,0:T(8,128)(2,1)}) %all-gather.25.cloned.1.call-update) | async-done | bytes 4718608 | tf_op jit(solution)/shard_map/all_gather | solution.py:505
  172.4 64.1 %all-gather.27.cloned.1.call-done.all_refs_8_ = bf16[3072,768]{1,0:T(8,128)(2,1)} async-done(((bf16[1536,768]{1,0:T(8,128)(2,1)}), bf16[3072,768]{1,0:T(8,128)(2,1)}) %all-gather.27.cloned.1.call-update) | async-done | bytes 4718608 | tf_op jit(solution)/shard_map/all_gather | solution.py:505
  236.4 151.6 %encoder_layer.1 = (bf16[1024,768]{1,0:T(8,128)(2,1)}, bf16[1024,768]{1,0:T(8,128)(2,1)}, bf16[768,3072]{1,0:T(8,128)(2,1)}, bf16[3072,768]{1,0:T(8,128)(2,1)}, ...) custom-call(bf16[1024,768]{1,0:T(8,128)(2,1)} %all_refs_0_.1, ...), custom_call_target="tpu_custom_call" | custom-call | tf_op jit(solution)/shard_map/encoder_layer/pallas_call | solution.py:484
  388.1 5.0 bitcast_convert_fusion
  396.4 7.3 convert_element_type.44
  403.7 6.7 convert_element_type.45
  410.5 17.5 %reduce-scatter.11.cloned.1.call-done = f32[384,768]{1,0:T(8,128)} async-done(((f32[768,768]{1,0:T(8,128)}), f32[384,768]{1,0:T(8,128)}) %reduce-scatter.11.cloned.1.call-update) | async-done | bytes 1179664 | tf_op jit(solution)/shard_map/reduce_scatter | solution.py:527
  428.0 37.1 %reduce-scatter.7.cloned.1.call-done = f32[384,768]{1,0:T(8,128)} async-done(((f32[768,768]{1,0:T(8,128)}), f32[384,768]{1,0:T(8,128)}) %reduce-scatter.7.cloned.1.call-update) | async-done | bytes 1179664 | tf_op jit(solution)/shard_map/reduce_scatter | solution.py:527
  465.1 37.0 %reduce-scatter.9.cloned.1.call-done = f32[384,768]{1,0:T(8,128)} async-done(((f32[768,768]{1,0:T(8,128)}), f32[384,768]{1,0:T(8,128)}) %reduce-scatter.9.cloned.1.call-update) | async-done | bytes 1179664 | tf_op jit(solution)/shard_map/reduce_scatter | solution.py:527
  502.1 36.9 %reduce-scatter.13.cloned.1.call-done = f32[384,768]{1,0:T(8,128)} async-done(((f32[768,768]{1,0:T(8,128)}), f32[384,768]{1,0:T(8,128)}) %reduce-scatter.13.cloned.1.call-update) | async-done | bytes 1179664 | tf_op jit(solution)/shard_map/reduce_scatter | solution.py:527
  539.0 112.9 %reduce-scatter.15.cloned.1.call-done = f32[384,3072]{1,0:T(8,128)} async-done(((f32[768,3072]{1,0:T(8,128)}), f32[384,3072]{1,0:T(8,128)}) %reduce-scatter.15.cloned.1.call-update) | async-done | bytes 4718608 | tf_op jit(solution)/shard_map/reduce_scatter | solution.py:527
  651.9 112.7 %reduce-scatter.17.cloned.1.call-done = f32[1536,768]{1,0:T(8,128)} async-done(((f32[3072,768]{1,0:T(8,128)}), f32[1536,768]{1,0:T(8,128)}) %reduce-scatter.17.cloned.1.call-update) | async-done | bytes 4718608 | tf_op jit(solution)/shard_map/reduce_scatter | solution.py:527
  767.4 7.5 all-reduce.12
  775.6 62.9 %all-reduce.10 = (f32[384]{0:T(512)}, f32[384]{0:T(512)}, f32[384]{0:T(512)}, f32[384]{0:T(512)}, f32[384]{0:T(512)}, /*index=5*/f32[384]{0:T(512)}, f32[384]{0:...) all-reduce(f32[384]{0:T(512)S(1)} %dynamic-slice.1, ...), channel_id=1, replica_groups=mesh['rep'=16,'shard'=2] {'rep'}, use_global_device_ids=true, to_apply=%region_1.0 | all-reduce | flops 4992 | bytes 39936 | tf_op jit(solution)/shard_map/psum | solution.py:528
  838.5 192.3 %all-reduce.15.cloned.1.call-done = (f32[384,768]{1,0:T(8,128)}, f32[384,768]{1,0:T(8,128)}, f32[384,768]{1,0:T(8,128)}, f32[384,768]{1,0:T(8,128)}, f32[384,3072]{1,0:T(8,128)}, /*index=5*/f32[1536,768]{1,0:T(8,128)}) async-done(((f32[384,768]{1,0:T(8,128)}, f32[384,768]{1,0:T(8,128)}, f32[384,768]{1,0:T(8,128)}, f32[384,768]{1,0:T(8,128)}, f32[384,3072]{1,0:T(8,128)}, /*index=5*/f32[1536,768]{1,0:T(8,128)}), ...) | async-done | bytes 14155792 | tf_op jit(solution)/shard_map/psum | solution.py:528
  (122 shorter events, 37.0 us)
Async XLA Ops:
  7.2 49.4 %all-gather.17.cloned.1.call-start = ((), (), s32[]{:S(2)}) async-start(), calls=%async_computation.6 | async-start | bytes 1769472 | tf_op jit(solution)/shard_map/all_gather | solution.py:505
  7.9 51.7 %all-gather.19.cloned.1.call-start = ((), (), s32[]{:S(2)}) async-start(), calls=%async_computation.7 | async-start | bytes 1769472 | tf_op jit(solution)/shard_map/all_gather | solution.py:505
  8.7 75.4 %all-gather.21.cloned.1.call-start = ((), (), s32[]{:S(2)}) async-start(), calls=%async_computation.8 | async-start | bytes 1769472 | tf_op jit(solution)/shard_map/all_gather | solution.py:505
  9.4 98.9 %all-gather.23.cloned.1.call-start = ((), (), s32[]{:S(2)}) async-start(), calls=%async_computation.9 | async-start | bytes 1769472 | tf_op jit(solution)/shard_map/all_gather | solution.py:505
  10.1 1.4 copy-start.14
  10.1 1.4 copy-start.15
  10.1 1.4 copy-start.6
  10.1 162.3 %all-gather.25.cloned.1.call-start = ((), (), s32[]{:S(2)}) async-start(), calls=%async_computation.10 | async-start | bytes 7077888 | tf_op jit(solution)/shard_map/all_gather | solution.py:505
  10.7 225.8 %all-gather.27.cloned.1.call-start = ((), (), s32[]{:S(2)}) async-start(), calls=%async_computation.11 | async-start | bytes 7077888 | tf_op jit(solution)/shard_map/all_gather | solution.py:505
  11.3 416.8 %reduce-scatter.11.cloned.1.call-start = ((), (), s32[]{:S(2)}) async-start(), calls=%async_computation.14 | async-start | bytes 3538944 | tf_op jit(solution)/shard_map/reduce_scatter | solution.py:527
  393.2 71.9 %reduce-scatter.7.cloned.1.call-start = ((), (), s32[]{:S(2)}) async-start(), calls=%async_computation.12 | async-start | bytes 3538944 | tf_op jit(solution)/shard_map/reduce_scatter | solution.py:527
  393.2 1.5 copy-start.1
  393.9 108.2 %reduce-scatter.9.cloned.1.call-start = ((), (), s32[]{:S(2)}) async-start(), calls=%async_computation.13 | async-start | bytes 3538944 | tf_op jit(solution)/shard_map/reduce_scatter | solution.py:527
  394.7 144.4 %reduce-scatter.13.cloned.1.call-start = ((), (), s32[]{:S(2)}) async-start(), calls=%async_computation.15 | async-start | bytes 3538944 | tf_op jit(solution)/shard_map/reduce_scatter | solution.py:527
  396.3 255.6 %reduce-scatter.15.cloned.1.call-start = ((), (), s32[]{:S(2)}) async-start(), calls=%async_computation.16 | async-start | bytes 14155776 | tf_op jit(solution)/shard_map/reduce_scatter | solution.py:527
  403.7 361.0 %reduce-scatter.17.cloned.1.call-start = ((), (), s32[]{:S(2)}) async-start(), calls=%async_computation.17 | async-start | bytes 14155776 | tf_op jit(solution)/shard_map/reduce_scatter | solution.py:527
  410.5 620.3 %all-reduce.15.cloned.1.call-start = ((), (), s32[]{:S(2)}) async-start(), calls=%async_computation.18 | async-start | bytes 28311552 | tf_op jit(solution)/shard_map/psum | solution.py:528
  764.7 2.5 copy-start.5
  1030.8 2.5 copy-start.4
  1030.8 3.5 copy-start.3
  1030.8 4.5 copy-start.2
  1033.3 3.6 copy-start
  1035.3 3.8 slice-start
  1036.9 2.5 slice-start.1
  (8 other events, 10.1 us)
Sparse Core Ops, SparseCore 0:
  9.6 25.5 all-gather.16
  36.7 22.8 all-gather.18
  61.2 22.8 all-gather.20
  85.5 22.7 all-gather.22
  109.7 62.6 all-gather.24
  173.8 62.6 all-gather.26
  393.3 34.7 reduce-scatter.10
  430.4 34.6 reduce-scatter.6
  467.4 34.7 reduce-scatter.8
  504.3 34.6 reduce-scatter.12
  541.3 110.5 reduce-scatter.14
  654.1 110.5 reduce-scatter.16
  769.8 260.9 all-reduce.14
